TPU v7x, 32 devices: a whole 2x2x4 slice. The times are simulated.
32 devices in a mesh: row: 4 (over x, core), col: 8 (over z, y).
Axes of the slice: x: 2, y: 2, z: 4, core: 2. Of those that a mesh axis runs over, the one named last changes fastest.
Arguments:
- blocks: float32 [256, 8, 128, 128], P(('row', 'col')), may hold values from -2 to 2
- prolong: float32 [256, 128, 128], P(('row', 'col')), may hold values from -0.5 to 0.5
- counts: int32 [256], P(('row', 'col')), may hold values from 1 to 8
- columns: int32 [256, 8], P(('row', 'col')), may hold values from 0 to 63, as said below
- aggregates: int32 [256], P(('row', 'col')), may hold values from 0 to 1
Outputs:
- coarse_operator: float32 [64, 16, 128, 128], P(('row', 'col'))
Inputs may be any that keep to these rules, and one draw needn't show every extreme that they name: Over all slots of the 8 rows of one device, the columns that fall among the rows of any one device of the slab (columns // 8 equal) take at most 2 distinct values; every device reaches 2 for some such device.
All inputs are finite; a program needn't handle non-finite values.
Results may differ from a plain program's by a relative error of at most 0.0003.
Values sent between devices are 32-bit elements; how exact they have to be, the bound alone decides.
A program may use at most 64 MiB of HBM per device.

v0:
```python
import functools

import jax
import jax.numpy as jnp
from jax import lax
from jax.experimental import pallas as pl
from jax.experimental.pallas import tpu as pltpu
from jax.sharding import PartitionSpec as P

AGD = 2
CAP = 2
F32 = jnp.float32
BF16 = jnp.bfloat16
I32 = jnp.int32


def halves(x):
    high = x.astype(BF16)
    return high, (x - high.astype(F32)).astype(BF16)


def dot(a, b):
    return jnp.dot(a, b, preferred_element_type=F32)


def kernel(
    n, m, blocks_ref, prolong_ref, cols_ref, agg_ref, counts_ref,
    out_ref, bound_ref,
    cols_v, agg_v, cols_s, agg_s, counts_s, small_sem,
    blocks, prolong, partial, table, sent, got, cols_all, agg_all, rowsum, peak, peaks_col,
    peak2, peaks_row, table_s,
    block_sem, prolong_sem, table_sem, cols_send, cols_recv, agg_send, agg_recv,
    tile_send, tile_recv, pc_send, pc_recv, pr_send, pr_recv,
):
    rows, slots = cols_v.shape
    tile = prolong.shape[-1]
    none = rows * slots
    me = lax.axis_index("col")
    my_row = lax.axis_index("row")

    load_prolong = pltpu.make_async_copy(prolong_ref, prolong, prolong_sem)
    small = [
        pltpu.make_async_copy(src, dst, small_sem.at[at])
        for at, (src, dst) in enumerate(
            (
                (cols_ref, cols_v),
                (agg_ref, agg_v),
                (cols_ref, cols_s),
                (agg_ref, agg_s),
                (counts_ref, counts_s),
            )
        )
    ]
    for copy in small:
        copy.start()
    load_prolong.start()

    def load_block(i):
        return pltpu.make_async_copy(blocks_ref.at[i], blocks.at[i], block_sem.at[i])

    @pl.loop(0, rows)
    def _(i):
        load_block(i).start()

    def across(off):
        return lax.rem(me + off, n)

    def below(off):
        return lax.rem(my_row + off, m)

    barrier = pltpu.get_barrier_semaphore()

    @pl.loop(1, n)
    def _(off):
        pl.semaphore_signal(barrier, inc=1, device_id={"col": across(off)})

    @pl.loop(1, m)
    def _(off):
        pl.semaphore_signal(barrier, inc=1, device_id={"row": below(off)})

    for copy in small:
        copy.wait()
    pl.semaphore_wait(barrier, n + m - 2)

    def far_first(t):
        return n // 2 + (lax.rem(t, 2) * 2 - 1) * (t // 2)

    def send_cols(to, slot):
        return pltpu.make_async_remote_copy(
            cols_v, cols_all.at[slot], cols_send.at[to], cols_recv.at[slot], device_id={"col": to}
        )

    def send_agg(to, slot):
        return pltpu.make_async_remote_copy(
            agg_v, agg_all.at[slot], agg_send.at[to], agg_recv.at[slot], device_id={"col": to}
        )

    @pl.loop(1, n)
    def _(t):
        to = across(far_first(t))
        send_cols(to, me).start()

    @pl.loop(1, n)
    def _(t):
        send_agg(across(far_first(t)), me).start()

    sub = lax.broadcasted_iota(I32, (8, 128), 0)
    lane = lax.broadcasted_iota(I32, (8, 128), 1)
    keys = jnp.full((8, 128), -1, I32)
    for i in range(rows):
        for k in range(slots):
            here = (sub == i) & (lane == k)
            keys = jnp.where(here, cols_s[i, k] * AGD + agg_s[0, i], keys)
    order = sub * slots + lane

    def scan_keys(i, carry):
        prev, low, high = carry
        for k in range(slots):
            col = cols_s[i, k]
            s = i * slots + k
            owner, within = col // rows, lax.rem(col, rows)
            key = jnp.where(k < counts_s[0, i], col * AGD + agg_s[0, i], -2)
            prev = jnp.where((keys == key) & (order > s), s, prev)
            low = jnp.where(lane == owner, jnp.minimum(low, within), low)
            high = jnp.where(lane == owner, jnp.maximum(high, within), high)
        return prev, low, high

    prev, low, high = lax.fori_loop(
        0, rows, scan_keys,
        (jnp.full((8, 128), none, I32), jnp.full((8, 128), rows - 1, I32), jnp.zeros((8, 128), I32)),
    )
    wanted = jnp.where(lax.rem(sub, 2) == 0, low, jnp.where(high > low, high, -1))

    def scan_last(i, last):
        for k in range(slots):
            col = cols_s[i, k]
            owner, within = col // rows, lax.rem(col, rows)
            row = jnp.where(k < counts_s[0, i], agg_s[0, i], -1)
            hit = (lane == owner) & (sub // 2 == row) & (wanted == within)
            last = jnp.where(hit, i * slots + k, last)
        return last

    last = lax.fori_loop(0, rows, scan_last, jnp.full((8, 128), none, I32))
    table[0:8, :] = prev
    table[8:16, :] = last
    table[16:24, :] = jnp.where(sub == 0, low, high)
    to_scalars = pltpu.make_async_copy(table, table_s, table_sem)
    to_scalars.start()
    partial[none] = jnp.zeros((tile, tile), F32)
    agg_all[me] = agg_v[...]
    to_scalars.wait()

    load_prolong.wait()
    got[me, 0] = prolong[table_s[16, me]]
    got[me, 1] = prolong[table_s[17, me]]

    def send_tiles(to, slot):
        return pltpu.make_async_remote_copy(
            sent.at[to], got.at[slot], tile_send.at[to], tile_recv.at[slot], device_id={"col": to}
        )

    def reply(t, _):
        to = across(far_first(t))
        send_cols(to, to).wait_recv()
        asked = cols_all[to]
        mine = asked // rows == me
        within = lax.rem(asked, rows)
        sent[to, 0] = prolong[jnp.min(jnp.where(mine, within, rows - 1))]
        sent[to, 1] = prolong[jnp.max(jnp.where(mine, within, 0))]
        send_tiles(to, me).start()
        return 0

    lax.fori_loop(1, n, reply, 0)

    def first_product(i, _):
        load_block(i).wait()
        ph, pw = halves(prolong[i].T)
        lhs = jnp.concatenate([ph, pw, ph], axis=1)
        for k in range(0, slots, 2):
            ah, aw = halves(blocks[i, k])
            bh, bw = halves(blocks[i, k + 1])
            highs = jnp.concatenate([ah, bh], axis=1)
            rhs = jnp.concatenate([highs, highs, jnp.concatenate([aw, bw], axis=1)], axis=0)
            both = dot(lhs, rhs)
            s = i * slots + k
            partial[s] = both[:, :tile] + partial[table_s[i, k]]
            partial[s + 1] = both[:, tile:] + partial[table_s[i, k + 1]]
        return 0

    lax.fori_loop(0, rows, first_product, 0)

    rowsum[...] = jnp.zeros_like(rowsum)
    spot = lax.broadcasted_iota(I32, agg_v.shape, 1)

    def second_product(owner):
        lhs = jnp.concatenate(
            [
                jnp.concatenate([partial[table_s[8 + c * CAP + r, owner]] for r in range(CAP)], axis=1)
                for c in range(AGD)
            ],
            axis=0,
        )
        ids = agg_all[owner]
        right = []
        for r in range(CAP):
            one = jnp.max(jnp.where(spot == table_s[16 + r, owner], ids, 0)).astype(F32)
            p = got[owner, r]
            right.append(jnp.concatenate([p * (1.0 - one), p * one], axis=1))
        rhs = jnp.concatenate(right, axis=0)
        lh, lw = halves(lhs)
        rh, rw = halves(rhs)
        prod = dot(lh, rh) + dot(lh, rw) + dot(lw, rh)
        size = jnp.abs(prod)
        rowsum[...] += size[:, :tile] + size[:, tile:]
        for c in range(AGD):
            for a in range(AGD):
                out_ref[c, owner * AGD + a] = prod[
                    c * tile : (c + 1) * tile, a * tile : (a + 1) * tile
                ]

    second_product(me)

    def collect(t, _):
        owner = lax.rem(me - far_first(t) + n, n)
        send_agg(owner, owner).wait_recv()
        send_tiles(owner, owner).wait_recv()
        second_product(owner)
        return 0

    lax.fori_loop(1, n, collect, 0)

    most = jnp.max(jnp.sum(rowsum[...], axis=1, keepdims=True), axis=0, keepdims=True)
    peak[...] = jnp.broadcast_to(most, peak.shape)
    peaks_col[me] = jnp.broadcast_to(most, peak.shape)

    def send_peak(to, slot):
        return pltpu.make_async_remote_copy(
            peak, peaks_col.at[slot], pc_send.at[to], pc_recv.at[slot], device_id={"col": to}
        )

    def send_peak2(to, slot):
        return pltpu.make_async_remote_copy(
            peak2, peaks_row.at[slot], pr_send.at[to], pr_recv.at[slot], device_id={"row": to}
        )

    @pl.loop(1, n)
    def _(t):
        send_peak(across(far_first(t)), me).start()

    @pl.loop(1, n)
    def _(off):
        to = across(off)
        send_cols(to, me).wait_send()
        send_agg(to, me).wait_send()
        send_tiles(to, me).wait_send()

    @pl.loop(1, n)
    def _(off):
        send_peak(across(off), across(off)).wait_recv()

    over = jnp.max(peaks_col[...], axis=0)
    peak2[...] = over
    peaks_row[my_row] = over

    @pl.loop(1, m)
    def _(off):
        send_peak2(below(off), my_row).start()

    @pl.loop(1, m)
    def _(off):
        send_peak2(below(off), below(off)).wait_recv()

    bound_ref[...] = jnp.broadcast_to(
        jnp.max(peaks_row[...], axis=0)[:1, :1] + 1e-06, bound_ref.shape
    )

    @pl.loop(1, n)
    def _(off):
        send_peak(across(off), me).wait_send()

    @pl.loop(1, m)
    def _(off):
        send_peak2(below(off), my_row).wait_send()


def per_device(blocks, prolong, counts, columns, aggregates):
    rows, slots, tile, _ = blocks.shape
    n, m = lax.axis_size("col"), lax.axis_size("row")
    agg_row = aggregates.reshape(1, rows)
    dma = pltpu.SemaphoreType.DMA
    vmem = pl.BlockSpec(memory_space=pltpu.VMEM)
    hbm = pl.BlockSpec(memory_space=pltpu.HBM)
    galerkin, bound = pl.pallas_call(
        functools.partial(kernel, n, m),
        name="galerkin",
        out_shape=(
            jax.ShapeDtypeStruct((AGD, AGD * n, tile, tile), F32),
            jax.ShapeDtypeStruct((tile, tile), F32),
        ),
        in_specs=[hbm] * 5,
        out_specs=(vmem, vmem),
        scratch_shapes=[
            pltpu.VMEM((rows, slots), I32),
            pltpu.VMEM((1, rows), I32),
            pltpu.SMEM((rows, slots), I32),
            pltpu.SMEM((1, rows), I32),
            pltpu.SMEM((1, rows), I32),
            dma((5,)),
            pltpu.VMEM((rows, slots, tile, tile), F32),
            pltpu.VMEM((rows, tile, tile), F32),
            pltpu.VMEM((rows * slots + 1, tile, tile), F32),
            pltpu.VMEM((24, 128), I32),
            pltpu.VMEM((n, CAP, tile, tile), F32),
            pltpu.VMEM((n, CAP, tile, tile), F32),
            pltpu.VMEM((n, rows, slots), I32),
            pltpu.VMEM((n, 1, rows), I32),
            pltpu.VMEM((AGD * tile, tile), F32),
            pltpu.VMEM((8, 128), F32),
            pltpu.VMEM((n, 8, 128), F32),
            pltpu.VMEM((8, 128), F32),
            pltpu.VMEM((m, 8, 128), F32),
            pltpu.SMEM((24, 128), I32),
            dma((rows,)),
            dma,
            dma,
        ]
        + [dma((n,)) for _ in range(8)]
        + [dma((m,)) for _ in range(2)],
        compiler_params=pltpu.CompilerParams(
            collective_id=0, has_side_effects=True, vmem_limit_bytes=48 * 1024 * 1024
        ),
    )(*(pltpu.with_memory_space_constraint(x, pltpu.HBM) for x in (blocks, prolong, columns, agg_row, counts.reshape(1, rows))))
    return galerkin / bound


def solution(mesh):
    placed = (
        P(("row", "col"), None, None, None),
        P(("row", "col"), None, None),
        P(("row", "col")),
        P(("row", "col"), None),
        P(("row", "col")),
    )
    return jax.shard_map(
        per_device,
        mesh=mesh,
        in_specs=placed,
        out_specs=P(("row", "col"), None, None, None),
        check_vma=False,
    )
```

profile of v0, /device:TPU:0, one launch (start us, length us, event | category | flops | bytes accessed | tf_op | source)
XLA Modules:
  0.0 42.9 jit_solution(12592485697069654479)
XLA Ops:
  0.0 41.3 %galerkin.1 = (f32[2,16,128,128]{3,2,1,0:T(8,128)S(1)}, f32[128,128]{1,0:T(8,128)S(1)}) custom-call(f32[8,8,128,128]{3,2,1,0:T(8,128)} %blocks_ref.1, f32[8,128,128]{2,1,0:T(8,128)} %prolong_ref.1, s32[8,8]{1,0:T(8,128)} %cols_ref.1, s32[1,8]{1,0:T(1,128)} %bitcast.2, s32[1,8]{1,0:T(1,128)} %bitcast.3), custom_call_target="tpu_custom_call" | custom-call | tf_op jit(solution)/shard_map/galerkin/pallas_call | solution.py:293
  41.3 1.6 %broadcast_divide_fusion = f32[2,16,128,128]{3,2,1,0:T(8,128)} fusion(f32[2,16,128,128]{3,2,1,0:T(8,128)S(1)} %get-tuple-element.7, f32[128,128]{1,0:T(8,128)S(1)} %get-tuple-element.8), kind=kLoop, calls=%fused_computation | loop fusion | flops 524288 | bytes 4259840 | tf_op jit(solution)/shard_map/div | solution.py:333
where the time goes:
time: 43.1 us; the launch traced here: 42.9 us
  Pallas kernels  41.3 us (96%)
  other arithmetic  1.62 us (4%)
    pallas_call x1, Pallas kernels, per_device(): pl.pallas_call(functools.partial(kernel, n, m), name='galerkin', out_shap...  41.3 us
    div x1, other arithmetic, per_device(): return galerkin / bound  1.62 us

commit v1 on v0

v1 whole, which is shorter than its diff:
```python
import functools

import jax
import jax.numpy as jnp
from jax import lax
from jax.experimental import pallas as pl
from jax.experimental.pallas import tpu as pltpu
from jax.sharding import PartitionSpec as P

AGD = 2
CAP = 2
F32 = jnp.float32
BF16 = jnp.bfloat16
I32 = jnp.int32


def halves(x):
    high = x.astype(BF16)
    return high, (x - high.astype(F32)).astype(BF16)


def dot(a, b):
    return jnp.dot(a, b, preferred_element_type=F32)


def kernel(
    n, m, blocks_ref, prolong_ref, cols_ref, agg_ref, counts_ref,
    out_ref, bound_ref,
    ask, cols_s, agg_s, counts_s, small_sem,
    blocks, prolong, partial, table, sent, got, ask_all, rowsum, peak, peaks, table_s,
    block_sem, prolong_sem, table_sem, ask_send, ask_recv,
    tile_send, tile_recv, peak_send, peak_recv, known,
):
    rows, slots = cols_s.shape
    tile = prolong.shape[-1]
    none = rows * slots
    me = lax.axis_index("col")
    my_row = lax.axis_index("row")

    width = max(1, n // 4)
    length = n // width
    line, y = me // width, lax.rem(me, width)
    side = line // (length // 2)
    inward = 1 - 2 * side

    def each(distance, first, last, act):
        for way in (1, -1) if distance else (1,):
            z = line + way * distance * inward

            @pl.when((z >= 0) & (z < length))
            def _():
                @pl.loop(first, last)
                def _(off):
                    act(z * width + lax.rem(y + off, width))

    def across(off):
        return lax.rem(me + off, n)

    def below(off):
        return lax.rem(my_row + off, m)

    barrier = pltpu.get_barrier_semaphore()

    def greet(to):
        pl.semaphore_signal(barrier, inc=1, device_id={"col": to})

    each(1, 0, 1, greet)
    each(0, 1, width, greet)

    @pl.loop(1, m)
    def _(off):
        pl.semaphore_signal(barrier, inc=1, device_id={"row": below(off)})

    beside = (line > 0).astype(I32) + (line < length - 1).astype(I32)

    small = [
        pltpu.make_async_copy(src, dst, small_sem.at[at])
        for at, (src, dst) in enumerate(
            (
                (cols_ref, ask.at[pl.ds(0, rows)]),
                (agg_ref, ask.at[pl.ds(rows, 1)]),
                (cols_ref, cols_s),
                (agg_ref, agg_s),
                (counts_ref, counts_s),
            )
        )
    ]
    load_prolong = pltpu.make_async_copy(prolong_ref, prolong, prolong_sem)
    for copy in small:
        copy.start()
    load_prolong.start()

    def load_block(i):
        return pltpu.make_async_copy(blocks_ref.at[i], blocks.at[i], block_sem.at[i])

    @pl.loop(0, rows)
    def _(i):
        load_block(i).start()

    for copy in small:
        copy.wait()
    pl.semaphore_wait(barrier, beside + width - 1 + m - 1)

    def send_ask(to, slot):
        return pltpu.make_async_remote_copy(
            ask, ask_all.at[slot], ask_send.at[to], ask_recv.at[slot], device_id={"col": to}
        )

    def send_tiles(to, slot):
        return pltpu.make_async_remote_copy(
            sent.at[to], got.at[slot], tile_send.at[to], tile_recv.at[slot], device_id={"col": to}
        )

    def ask_for(to):
        send_ask(to, me).start()

    def tell():
        @pl.when(line > 0)
        def _():
            pl.semaphore_signal(known.at[1], inc=1, device_id={"col": me - width})

        @pl.when(line < length - 1)
        def _():
            pl.semaphore_signal(known.at[0], inc=1, device_id={"col": me + width})

    def hear():
        @pl.when(line > 0)
        def _():
            pl.semaphore_wait(known.at[0], 1)

        @pl.when(line < length - 1)
        def _():
            pl.semaphore_wait(known.at[1], 1)

    tell()
    each(1, 0, 1, ask_for)
    each(0, 1, width, ask_for)
    for distance in range(1, length):
        hear()
        if distance < length - 1:
            tell()
        each(distance, 1, width, ask_for)
        if distance < length - 1:
            each(distance + 1, 0, 1, ask_for)

    load_prolong.wait()

    def reply(to):
        send_ask(to, to).wait_recv()
        asked = ask_all[to][:rows]
        mine = asked // rows == me
        within = lax.rem(asked, rows)
        sent[to, 0] = prolong[jnp.min(jnp.where(mine, within, rows - 1))]
        sent[to, 1] = prolong[jnp.max(jnp.where(mine, within, 0))]
        send_tiles(to, me).start()

    each(0, 1, width, reply)
    for distance in range(1, length):
        each(distance, 0, 1, reply)
        each(distance, 1, width, reply)

    sub = lax.broadcasted_iota(I32, (8, 128), 0)
    lane = lax.broadcasted_iota(I32, (8, 128), 1)
    keys = jnp.full((8, 128), -1, I32)
    for i in range(rows):
        for k in range(slots):
            here = (sub == i) & (lane == k)
            keys = jnp.where(here, cols_s[i, k] * AGD + agg_s[0, i], keys)
    order = sub * slots + lane

    def scan_keys(i, carry):
        prev, low, high = carry
        for k in range(slots):
            col = cols_s[i, k]
            s = i * slots + k
            owner, within = col // rows, lax.rem(col, rows)
            key = jnp.where(k < counts_s[0, i], col * AGD + agg_s[0, i], -2)
            prev = jnp.where((keys == key) & (order > s), s, prev)
            low = jnp.where(lane == owner, jnp.minimum(low, within), low)
            high = jnp.where(lane == owner, jnp.maximum(high, within), high)
        return prev, low, high

    prev, low, high = lax.fori_loop(
        0, rows, scan_keys,
        (jnp.full((8, 128), none, I32), jnp.full((8, 128), rows - 1, I32), jnp.zeros((8, 128), I32)),
    )
    wanted = jnp.where(lax.rem(sub, 2) == 0, low, jnp.where(high > low, high, -1))

    def scan_last(i, last):
        for k in range(slots):
            col = cols_s[i, k]
            owner, within = col // rows, lax.rem(col, rows)
            row = jnp.where(k < counts_s[0, i], agg_s[0, i], -1)
            hit = (lane == owner) & (sub // 2 == row) & (wanted == within)
            last = jnp.where(hit, i * slots + k, last)
        return last

    last = lax.fori_loop(0, rows, scan_last, jnp.full((8, 128), none, I32))
    table[0:8, :] = prev
    table[8:16, :] = last
    table[16:24, :] = jnp.where(sub == 0, low, high)
    to_scalars = pltpu.make_async_copy(table, table_s, table_sem)
    to_scalars.start()
    partial[none] = jnp.zeros((tile, tile), F32)
    ask_all[me] = ask[...]
    rowsum[...] = jnp.zeros_like(rowsum)
    to_scalars.wait()

    got[me, 0] = prolong[table_s[16, me]]
    got[me, 1] = prolong[table_s[17, me]]

    def first_product(i, _):
        load_block(i).wait()
        ph, pw = halves(prolong[i].T)
        lhs = jnp.concatenate([ph, pw, ph], axis=1)
        for k in range(0, slots, 2):
            ah, aw = halves(blocks[i, k])
            bh, bw = halves(blocks[i, k + 1])
            highs = jnp.concatenate([ah, bh], axis=1)
            rhs = jnp.concatenate([highs, highs, jnp.concatenate([aw, bw], axis=1)], axis=0)
            both = dot(lhs, rhs)
            s = i * slots + k
            partial[s] = both[:, :tile] + partial[table_s[i, k]]
            partial[s + 1] = both[:, tile:] + partial[table_s[i, k + 1]]
        return 0

    lax.fori_loop(0, rows, first_product, 0)

    spot = lax.broadcasted_iota(I32, (1, rows), 1)

    def second_product(owner):
        lhs = jnp.concatenate(
            [
                jnp.concatenate([partial[table_s[8 + c * CAP + r, owner]] for r in range(CAP)], axis=1)
                for c in range(AGD)
            ],
            axis=0,
        )
        ids = ask_all[owner][rows:]
        right = []
        for r in range(CAP):
            one = jnp.max(jnp.where(spot == table_s[16 + r, owner], ids, 0)).astype(F32)
            p = got[owner, r]
            right.append(jnp.concatenate([p * (1.0 - one), p * one], axis=1))
        rhs = jnp.concatenate(right, axis=0)
        lh, lw = halves(lhs)
        rh, rw = halves(rhs)
        prod = dot(lh, rh) + dot(lh, rw) + dot(lw, rh)
        size = jnp.abs(prod)
        rowsum[...] += size[:, :tile] + size[:, tile:]
        for c in range(AGD):
            for a in range(AGD):
                out_ref[c, owner * AGD + a] = prod[
                    c * tile : (c + 1) * tile, a * tile : (a + 1) * tile
                ]

    second_product(me)

    def collect(owner):
        send_tiles(owner, owner).wait_recv()
        second_product(owner)

    @pl.loop(1, n)
    def _(t):
        far = t // width
        own = line // (length // 2) * (length // 2)
        z = jnp.where(
            far < length // 2,
            own + lax.rem(line - own + far, length // 2),
            jnp.where(side == 0, length - 1 - (far - length // 2), far - length // 2),
        )
        collect(z * width + lax.rem(y + t, width))

    most = jnp.max(jnp.sum(rowsum[...], axis=1, keepdims=True), axis=0, keepdims=True)
    place_all = my_row * n + me
    peak[...] = jnp.broadcast_to(most, peak.shape)
    peaks[place_all] = jnp.broadcast_to(most, peak.shape)

    def far_first(t):
        down = n - t - (n - t <= me).astype(I32)
        return jnp.where(side == 0, down, t - 1 + (t - 1 >= me).astype(I32))

    def send_peak(row, col):
        return pltpu.make_async_remote_copy(
            peak, peaks.at[place_all], peak_send, peak_recv, device_id={"row": row, "col": col}
        )

    @pl.loop(1, n)
    def _(t):
        @pl.loop(0, m)
        def _(off):
            send_peak(below(off), far_first(t)).start()

    @pl.loop(1, m)
    def _(off):
        send_peak(below(off), me).start()

    @pl.loop(1, n)
    def _(off):
        to = across(off)
        send_ask(to, me).wait_send()
        send_tiles(to, me).wait_send()

    others = pl.ds(0, n * m - 1)
    every = pltpu.make_async_remote_copy(
        peaks.at[others], peaks.at[others], peak_send, peak_recv, device_id={"col": across(1)}
    )
    every.wait_send()
    every.wait_recv()
    bound_ref[...] = jnp.broadcast_to(
        jnp.max(peaks[...], axis=0)[:1, :1] + 1e-06, bound_ref.shape
    )


def per_device(blocks, prolong, counts, columns, aggregates):
    rows, slots, tile, _ = blocks.shape
    n, m = lax.axis_size("col"), lax.axis_size("row")
    agg_row = aggregates.reshape(1, rows)
    dma = pltpu.SemaphoreType.DMA
    vmem = pl.BlockSpec(memory_space=pltpu.VMEM)
    hbm = pl.BlockSpec(memory_space=pltpu.HBM)
    galerkin, bound = pl.pallas_call(
        functools.partial(kernel, n, m),
        name="galerkin",
        out_shape=(
            jax.ShapeDtypeStruct((AGD, AGD * n, tile, tile), F32),
            jax.ShapeDtypeStruct((tile, tile), F32),
        ),
        in_specs=[hbm] * 5,
        out_specs=(vmem, vmem),
        scratch_shapes=[
            pltpu.VMEM((rows + 1, slots), I32),
            pltpu.SMEM((rows, slots), I32),
            pltpu.SMEM((1, rows), I32),
            pltpu.SMEM((1, rows), I32),
            dma((5,)),
            pltpu.VMEM((rows, slots, tile, tile), F32),
            pltpu.VMEM((rows, tile, tile), F32),
            pltpu.VMEM((rows * slots + 1, tile, tile), F32),
            pltpu.VMEM((24, 128), I32),
            pltpu.VMEM((n, CAP, tile, tile), F32),
            pltpu.VMEM((n, CAP, tile, tile), F32),
            pltpu.VMEM((n, rows + 1, slots), I32),
            pltpu.VMEM((AGD * tile, tile), F32),
            pltpu.VMEM((1, 128), F32),
            pltpu.VMEM((n * m, 1, 128), F32),
            pltpu.SMEM((24, 128), I32),
            dma((rows,)),
            dma,
            dma,
            dma((n,)),
            dma((n,)),
            dma((n,)),
            dma((n,)),
            dma,
            dma,
            pltpu.SemaphoreType.REGULAR((2,)),
        ],
        compiler_params=pltpu.CompilerParams(
            collective_id=0, has_side_effects=True, vmem_limit_bytes=48 * 1024 * 1024
        ),
    )(*(pltpu.with_memory_space_constraint(x, pltpu.HBM) for x in (blocks, prolong, columns, agg_row, counts.reshape(1, rows))))
    return galerkin / bound


def solution(mesh):
    placed = (
        P(("row", "col"), None, None, None),
        P(("row", "col"), None, None),
        P(("row", "col")),
        P(("row", "col"), None),
        P(("row", "col")),
    )
    return jax.shard_map(
        per_device,
        mesh=mesh,
        in_specs=placed,
        out_specs=P(("row", "col"), None, None, None),
        check_vma=False,
    )
```

time: 43.1 us -> 39.8 us (0.923)
  Pallas kernels: 41.3 us -> 38 us
    pallas_call x1, Pallas kernels: 41.3 us -> 38 us  [per_device(): pl.pallas_call(functools.partial(kernel, n, m), name='galerkin', out_shap...]
where the time goes in v1:
time: 39.8 us; the launch traced here: 39.7 us
  Pallas kernels  38 us (95%)
  other arithmetic  1.62 us (4%)
    pallas_call x1, Pallas kernels, per_device(): pl.pallas_call(functools.partial(kernel, n, m), name='galerkin', out_shap...  38 us
    div x1, other arithmetic, per_device(): return galerkin / bound  1.62 us

profile of v1, /device:TPU:0, one launch (start us, length us, event | category | flops | bytes accessed | tf_op | source)
XLA Modules:
  0.0 39.7 jit_solution(13631566777996328968)
XLA Ops:
  0.0 38.0 %galerkin.1 = (f32[2,16,128,128]{3,2,1,0:T(8,128)S(1)}, f32[128,128]{1,0:T(8,128)S(1)}) custom-call(f32[8,8,128,128]{3,2,1,0:T(8,128)} %blocks_ref.1, f32[8,128,128]{2,1,0:T(8,128)} %prolong_ref.1, s32[8,8]{1,0:T(8,128)} %cols_ref.1, s32[1,8]{1,0:T(1,128)} %bitcast.2, s32[1,8]{1,0:T(1,128)} %bitcast.3), custom_call_target="tpu_custom_call" | custom-call | tf_op jit(solution)/shard_map/galerkin/pallas_call | solution.py:322
  38.0 1.6 %broadcast_divide_fusion = f32[2,16,128,128]{3,2,1,0:T(8,128)} fusion(f32[2,16,128,128]{3,2,1,0:T(8,128)S(1)} %get-tuple-element.7, f32[128,128]{1,0:T(8,128)S(1)} %get-tuple-element.8), kind=kLoop, calls=%fused_computation | loop fusion | flops 524288 | bytes 4259840 | tf_op jit(solution)/shard_map/div | solution.py:363

commit v2 on v1

--- a/solution.py
+++ b/solution.py
@@ -27,31 +27,30 @@
     n, m, blocks_ref, prolong_ref, cols_ref, agg_ref, counts_ref,
     out_ref, bound_ref,
     ask, cols_s, agg_s, counts_s, small_sem,
-    blocks, prolong, partial, table, sent, got, ask_all, rowsum, peak, peaks, table_s,
+    blocks, prolong, partial, table, sent, got, pushed, passed, ask_all, rowsum, peak, peaks, table_s,
     block_sem, prolong_sem, table_sem, ask_send, ask_recv,
-    tile_send, tile_recv, peak_send, peak_recv, known,
+    tile_send, tile_recv, relay_send, relay_recv, push_send, push_recv,
+    peak_send, peak_recv, known,
 ):
     rows, slots = cols_s.shape
     tile = prolong.shape[-1]
     none = rows * slots
+    cut = tile * 3 // 8
+    lead = tile // 4
     me = lax.axis_index("col")
     my_row = lax.axis_index("row")
 
-    width = max(1, n // 4)
-    length = n // width
+    width = n // 4
     line, y = me // width, lax.rem(me, width)
-    side = line // (length // 2)
-    inward = 1 - 2 * side
-
-    def each(distance, first, last, act):
-        for way in (1, -1) if distance else (1,):
-            z = line + way * distance * inward
-
-            @pl.when((z >= 0) & (z < length))
-            def _():
-                @pl.loop(first, last)
-                def _(off):
-                    act(z * width + lax.rem(y + off, width))
+    side = line // 2
+    outer = lax.rem(line + side, 2) == 0
+    inner = lax.rem(line + side, 2) == 1
+
+    def own(far, off):
+        return jnp.where(side == 1, 2 + far, 1 - far) * width + lax.rem(y + off, width)
+
+    def facing(far, off):
+        return jnp.where(side == 1, 1 - far, 2 + far) * width + lax.rem(y + off, width)
 
     def across(off):
         return lax.rem(me + off, n)
@@ -59,19 +58,28 @@
     def below(off):
         return lax.rem(my_row + off, m)
 
+    def each(where, far, first, act):
+        @pl.loop(first, width)
+        def _(off):
+            act(where(far, off))
+
     barrier = pltpu.get_barrier_semaphore()
 
     def greet(to):
         pl.semaphore_signal(barrier, inc=1, device_id={"col": to})
 
-    each(1, 0, 1, greet)
-    each(0, 1, width, greet)
+    @pl.when(inner)
+    def _():
+        greet(facing(0, 0))
+        greet(own(1, 0))
+
+    @pl.loop(1, width)
+    def _(off):
+        greet(line * width + lax.rem(y + off, width))
 
     @pl.loop(1, m)
     def _(off):
         pl.semaphore_signal(barrier, inc=1, device_id={"row": below(off)})
-
-    beside = (line > 0).astype(I32) + (line < length - 1).astype(I32)
 
     small = [
         pltpu.make_async_copy(src, dst, small_sem.at[at])
@@ -86,78 +94,130 @@
         )
     ]
     load_prolong = pltpu.make_async_copy(prolong_ref, prolong, prolong_sem)
+    load_prolong.start()
     for copy in small:
         copy.start()
-    load_prolong.start()
 
     def load_block(i):
         return pltpu.make_async_copy(blocks_ref.at[i], blocks.at[i], block_sem.at[i])
+
+    def send_ask(to, slot):
+        return pltpu.make_async_remote_copy(
+            ask, ask_all.at[slot], ask_send.at[to], ask_recv.at[slot], device_id={"col": to}
+        )
+
+    def send_push(part):
+        some = (pl.ds(0, lead), pl.ds(lead, cut - lead))[part]
+        return pltpu.make_async_remote_copy(
+            prolong_ref.at[:, some], pushed.at[:, some], push_send.at[part], push_recv.at[part],
+            device_id={"col": facing(0, 0)},
+        )
+
+    def send_tiles(to, slot):
+        return pltpu.make_async_remote_copy(
+            sent.at[to], got.at[slot], tile_send.at[to], tile_recv.at[slot], device_id={"col": to}
+        )
+
+    def send_rest(to, slot):
+        rest = pl.ds(cut, tile - cut)
+        return pltpu.make_async_remote_copy(
+            sent.at[to, :, rest], got.at[slot, :, rest], tile_send.at[to], tile_recv.at[slot],
+            device_id={"col": to},
+        )
+
+    def send_relay(to, slot):
+        return pltpu.make_async_remote_copy(
+            passed.at[to], got.at[slot, :, pl.ds(0, cut)], relay_send.at[to], relay_recv.at[slot],
+            device_id={"col": to},
+        )
+
+    def ask_for(to):
+        send_ask(to, me).start()
+
+    def tell(to, at):
+        pl.semaphore_signal(known.at[at], inc=1, device_id={"col": to})
+
+    pl.semaphore_wait(barrier, width + m - 1)
+
+    @pl.when(inner)
+    def _():
+        tell(facing(0, 0), 1)
+        send_push(0).start()
+
+    @pl.when(outer)
+    def _():
+        tell(own(0, 0), 0)
+
+    for copy in small:
+        copy.wait()
+
+    @pl.when(inner)
+    def _():
+        ask_for(facing(0, 0))
+        each(own, 0, 1, ask_for)
+        pl.semaphore_wait(known.at[0], 1)
+        tell(facing(0, 0), 1)
+        tell(own(1, 0), 0)
+        each(own, 1, 0, ask_for)
+        pl.semaphore_wait(known.at[1], 1)
+        tell(own(1, 0), 0)
+        each(facing, 0, 1, ask_for)
+        pl.semaphore_wait(known.at[1], 1)
+        tell(own(1, 0), 0)
+        each(facing, 1, 0, ask_for)
+        send_push(1).start()
+
+    @pl.when(outer)
+    def _():
+        ask_for(own(0, 0))
+        each(own, 1, 1, ask_for)
+        pl.semaphore_wait(known.at[0], 1)
+        ask_for(facing(0, 0))
+        each(own, 0, 1, ask_for)
+        pl.semaphore_wait(known.at[0], 1)
+        each(facing, 0, 1, ask_for)
+        pl.semaphore_wait(known.at[0], 1)
+        each(facing, 1, 0, ask_for)
 
     @pl.loop(0, rows)
     def _(i):
         load_block(i).start()
 
-    for copy in small:
-        copy.wait()
-    pl.semaphore_wait(barrier, beside + width - 1 + m - 1)
-
-    def send_ask(to, slot):
-        return pltpu.make_async_remote_copy(
-            ask, ask_all.at[slot], ask_send.at[to], ask_recv.at[slot], device_id={"col": to}
-        )
-
-    def send_tiles(to, slot):
-        return pltpu.make_async_remote_copy(
-            sent.at[to], got.at[slot], tile_send.at[to], tile_recv.at[slot], device_id={"col": to}
-        )
-
-    def ask_for(to):
-        send_ask(to, me).start()
-
-    def tell():
-        @pl.when(line > 0)
-        def _():
-            pl.semaphore_signal(known.at[1], inc=1, device_id={"col": me - width})
-
-        @pl.when(line < length - 1)
-        def _():
-            pl.semaphore_signal(known.at[0], inc=1, device_id={"col": me + width})
-
-    def hear():
-        @pl.when(line > 0)
-        def _():
-            pl.semaphore_wait(known.at[0], 1)
-
-        @pl.when(line < length - 1)
-        def _():
-            pl.semaphore_wait(known.at[1], 1)
-
-    tell()
-    each(1, 0, 1, ask_for)
-    each(0, 1, width, ask_for)
-    for distance in range(1, length):
-        hear()
-        if distance < length - 1:
-            tell()
-        each(distance, 1, width, ask_for)
-        if distance < length - 1:
-            each(distance + 1, 0, 1, ask_for)
-
     load_prolong.wait()
+
+    def bounds(to, owner):
+        asked = ask_all[to][:rows]
+        mine = asked // rows == owner
+        within = lax.rem(asked, rows)
+        return jnp.min(jnp.where(mine, within, rows - 1)), jnp.max(jnp.where(mine, within, 0))
 
     def reply(to):
         send_ask(to, to).wait_recv()
-        asked = ask_all[to][:rows]
-        mine = asked // rows == me
-        within = lax.rem(asked, rows)
-        sent[to, 0] = prolong[jnp.min(jnp.where(mine, within, rows - 1))]
-        sent[to, 1] = prolong[jnp.max(jnp.where(mine, within, 0))]
+        low, high = bounds(to, me)
+        sent[to, 0] = prolong[low]
+        sent[to, 1] = prolong[high]
         send_tiles(to, me).start()
 
-    each(0, 1, width, reply)
-    for distance in range(1, length):
-        each(distance, 0, 1, reply)
-        each(distance, 1, width, reply)
+    def reply_rest(to):
+        send_ask(to, to).wait_recv()
+        low, high = bounds(to, me)
+        sent[to, 0, cut:] = prolong[low][cut:]
+        sent[to, 1, cut:] = prolong[high][cut:]
+        send_rest(to, me).start()
+
+    @pl.when(inner)
+    def _():
+        each(own, 0, 1, reply)
+        each(own, 1, 0, reply)
+        each(facing, 1, 0, reply_rest)
+        each(facing, 0, 0, reply_rest)
+
+    @pl.when(outer)
+    def _():
+        each(own, 1, 1, reply)
+        each(own, 0, 0, reply)
+        each(facing, 1, 0, reply)
+        each(facing, 0, 0, reply)
 
     sub = lax.broadcasted_iota(I32, (8, 128), 0)
     lane = lax.broadcasted_iota(I32, (8, 128), 1)
@@ -208,6 +268,23 @@
 
     got[me, 0] = prolong[table_s[16, me]]
     got[me, 1] = prolong[table_s[17, me]]
+
+    @pl.when(inner)
+    def _():
+        send_push(0).wait_recv()
+        send_push(1).wait_recv()
+        face = facing(0, 0)
+
+        def relay(to):
+            low, high = bounds(to, face)
+            passed[to, 0] = pushed[low]
+            passed[to, 1] = pushed[high]
+            send_relay(to, face).start()
+
+        each(own, 0, 1, relay)
+        each(own, 1, 0, relay)
+        got[face, 0, :cut] = pushed[table_s[16, face]]
+        got[face, 1, :cut] = pushed[table_s[17, face]]
 
     def first_product(i, _):
         load_block(i).wait()
@@ -260,16 +337,34 @@
         send_tiles(owner, owner).wait_recv()
         second_product(owner)
 
-    @pl.loop(1, n)
-    def _(t):
-        far = t // width
-        own = line // (length // 2) * (length // 2)
-        z = jnp.where(
-            far < length // 2,
-            own + lax.rem(line - own + far, length // 2),
-            jnp.where(side == 0, length - 1 - (far - length // 2), far - length // 2),
-        )
-        collect(z * width + lax.rem(y + t, width))
+    def collect_parts(owner):
+        send_relay(owner, owner).wait_recv()
+        send_rest(owner, owner).wait_recv()
+        second_product(owner)
+
+    @pl.when(inner)
+    def _():
+        each(own, 0, 1, collect)
+        each(own, 1, 0, collect)
+
+    @pl.when(outer)
+    def _():
+        each(own, 1, 1, collect)
+        each(own, 0, 0, collect)
+
+    each(facing, 1, 0, collect)
+
+    @pl.when(inner)
+    def _():
+        send_rest(facing(0, 0), facing(0, 0)).wait_recv()
+
+    @pl.when(outer)
+    def _():
+        send_relay(facing(0, 0), facing(0, 0)).wait_recv()
+        send_rest(facing(0, 0), facing(0, 0)).wait_recv()
+
+    second_product(facing(0, 0))
+    each(facing, 0, 1, collect_parts)
 
     most = jnp.max(jnp.sum(rowsum[...], axis=1, keepdims=True), axis=0, keepdims=True)
     place_all = my_row * n + me
@@ -295,21 +390,47 @@
     def _(off):
         send_peak(below(off), me).start()
 
-    @pl.loop(1, n)
-    def _(off):
-        to = across(off)
-        send_ask(to, me).wait_send()
-        send_tiles(to, me).wait_send()
-
     others = pl.ds(0, n * m - 1)
     every = pltpu.make_async_remote_copy(
         peaks.at[others], peaks.at[others], peak_send, peak_recv, device_id={"col": across(1)}
     )
-    every.wait_send()
+
+    @pl.loop(1, n)
+    def _(off):
+        send_ask(across(off), me).wait_send()
+
+    def sent_whole(to):
+        send_tiles(to, me).wait_send()
+
+    def sent_rest(to):
+        send_rest(to, me).wait_send()
+
+    def sent_relay(to):
+        send_relay(to, me).wait_send()
+
+    @pl.when(inner)
+    def _():
+        send_push(0).wait_send()
+        send_push(1).wait_send()
+        each(own, 0, 1, sent_whole)
+        each(own, 0, 1, sent_relay)
+        each(own, 1, 0, sent_whole)
+        each(own, 1, 0, sent_relay)
+        each(facing, 0, 0, sent_rest)
+        each(facing, 1, 0, sent_rest)
+
+    @pl.when(outer)
+    def _():
+        each(own, 1, 1, sent_whole)
+        each(own, 0, 0, sent_whole)
+        each(facing, 0, 0, sent_whole)
+        each(facing, 1, 0, sent_whole)
+
     every.wait_recv()
     bound_ref[...] = jnp.broadcast_to(
         jnp.max(peaks[...], axis=0)[:1, :1] + 1e-06, bound_ref.shape
     )
+    every.wait_send()
 
 
 def per_device(blocks, prolong, counts, columns, aggregates):
@@ -340,6 +461,8 @@
             pltpu.VMEM((24, 128), I32),
             pltpu.VMEM((n, CAP, tile, tile), F32),
             pltpu.VMEM((n, CAP, tile, tile), F32),
+            pltpu.VMEM((rows, tile * 3 // 8, tile), F32),
+            pltpu.VMEM((n, CAP, tile * 3 // 8, tile), F32),
             pltpu.VMEM((n, rows + 1, slots), I32),
             pltpu.VMEM((AGD * tile, tile), F32),
             pltpu.VMEM((1, 128), F32),
@@ -352,6 +475,10 @@
             dma((n,)),
             dma((n,)),
             dma((n,)),
+            dma((n,)),
+            dma((n,)),
+            dma((2,)),
+            dma((2,)),
             dma,
             dma,
             pltpu.SemaphoreType.REGULAR((2,)),

time: 39.8 us -> 37.1 us (0.932)
  Pallas kernels: 38 us -> 35.4 us
    pallas_call x1, Pallas kernels: 38 us -> 35.4 us  [per_device(): pl.pallas_call(functools.partial(kernel, n, m), name='galerkin', out_shap...]
where the time goes in v2:
time: 37.1 us; the launch traced here: 37 us
  Pallas kernels  35.4 us (95%)
  other arithmetic  1.62 us (4%)
    pallas_call x1, Pallas kernels, per_device(): pl.pallas_call(functools.partial(kernel, n, m), name='galerkin', out_shap...  35.4 us
    div x1, other arithmetic, per_device(): return galerkin / bound  1.62 us

profile of v2, /device:TPU:0, one launch (start us, length us, event | category | flops | bytes accessed | tf_op | source)
XLA Modules:
  0.0 37.0 jit_solution(3119253774035155850)
XLA Ops:
  0.0 35.4 %galerkin.1 = (f32[2,16,128,128]{3,2,1,0:T(8,128)S(1)}, f32[128,128]{1,0:T(8,128)S(1)}) custom-call(f32[8,8,128,128]{3,2,1,0:T(8,128)} %blocks_ref.1, f32[8,128,128]{2,1,0:T(8,128)} %prolong_ref.1, s32[8,8]{1,0:T(8,128)} %cols_ref.1, s32[1,8]{1,0:T(1,128)} %bitcast.2, s32[1,8]{1,0:T(1,128)} %bitcast.3), custom_call_target="tpu_custom_call" | custom-call | tf_op jit(solution)/shard_map/galerkin/pallas_call | solution.py:443
  35.4 1.6 %broadcast_divide_fusion = f32[2,16,128,128]{3,2,1,0:T(8,128)} fusion(f32[2,16,128,128]{3,2,1,0:T(8,128)S(1)} %get-tuple-element.7, f32[128,128]{1,0:T(8,128)S(1)} %get-tuple-element.8), kind=kLoop, calls=%fused_computation | loop fusion | flops 524288 | bytes 4259840 | tf_op jit(solution)/shard_map/div | solution.py:490

commit v3 on v2

--- a/solution.py
+++ b/solution.py
@@ -35,7 +35,7 @@
     rows, slots = cols_s.shape
     tile = prolong.shape[-1]
     none = rows * slots
-    cut = tile * 3 // 8
+    cut = tile // 2
     lead = tile // 4
     me = lax.axis_index("col")
     my_row = lax.axis_index("row")
@@ -109,7 +109,7 @@
     def send_push(part):
         some = (pl.ds(0, lead), pl.ds(lead, cut - lead))[part]
         return pltpu.make_async_remote_copy(
-            prolong_ref.at[:, some], pushed.at[:, some], push_send.at[part], push_recv.at[part],
+            prolong.at[:, some], pushed.at[:, some], push_send.at[part], push_recv.at[part],
             device_id={"col": facing(0, 0)},
         )
 
@@ -142,6 +142,7 @@
     @pl.when(inner)
     def _():
         tell(facing(0, 0), 1)
+        load_prolong.wait()
         send_push(0).start()
 
     @pl.when(outer)
@@ -183,7 +184,9 @@
     def _(i):
         load_block(i).start()
 
-    load_prolong.wait()
+    @pl.when(outer)
+    def _():
+        load_prolong.wait()
 
     def bounds(to, owner):
         asked = ask_all[to][:rows]
@@ -371,24 +374,24 @@
     peak[...] = jnp.broadcast_to(most, peak.shape)
     peaks[place_all] = jnp.broadcast_to(most, peak.shape)
 
-    def far_first(t):
-        down = n - t - (n - t <= me).astype(I32)
-        return jnp.where(side == 0, down, t - 1 + (t - 1 >= me).astype(I32))
-
     def send_peak(row, col):
         return pltpu.make_async_remote_copy(
             peak, peaks.at[place_all], peak_send, peak_recv, device_id={"row": row, "col": col}
         )
 
-    @pl.loop(1, n)
-    def _(t):
-        @pl.loop(0, m)
-        def _(off):
-            send_peak(below(off), far_first(t)).start()
-
-    @pl.loop(1, m)
-    def _(off):
-        send_peak(below(off), me).start()
+    @pl.loop(0, n)
+    def _(col):
+        @pl.when(col != me)
+        def _():
+            @pl.loop(0, m)
+            def _(row):
+                send_peak(row, col).start()
+
+        @pl.when(col == me)
+        def _():
+            @pl.loop(1, m)
+            def _(off):
+                send_peak(below(off), me).start()
 
     others = pl.ds(0, n * m - 1)
     every = pltpu.make_async_remote_copy(
@@ -426,11 +429,11 @@
         each(facing, 0, 0, sent_whole)
         each(facing, 1, 0, sent_whole)
 
+    every.wait_send()
     every.wait_recv()
     bound_ref[...] = jnp.broadcast_to(
         jnp.max(peaks[...], axis=0)[:1, :1] + 1e-06, bound_ref.shape
     )
-    every.wait_send()
 
 
 def per_device(blocks, prolong, counts, columns, aggregates):
@@ -461,8 +464,8 @@
             pltpu.VMEM((24, 128), I32),
             pltpu.VMEM((n, CAP, tile, tile), F32),
             pltpu.VMEM((n, CAP, tile, tile), F32),
-            pltpu.VMEM((rows, tile * 3 // 8, tile), F32),
-            pltpu.VMEM((n, CAP, tile * 3 // 8, tile), F32),
+            pltpu.VMEM((rows, tile // 2, tile), F32),
+            pltpu.VMEM((n, CAP, tile // 2, tile), F32),
             pltpu.VMEM((n, rows + 1, slots), I32),
             pltpu.VMEM((AGD * tile, tile), F32),
             pltpu.VMEM((1, 128), F32),

time: 37.1 us -> 36.5 us (0.984)
  Pallas kernels: 35.4 us -> 34.7 us
    pallas_call x1, Pallas kernels: 35.4 us -> 34.7 us  [per_device(): pl.pallas_call(functools.partial(kernel, n, m), name='galerkin', out_shap...]
where the time goes in v3:
time: 36.5 us; the launch traced here: 36.3 us
  Pallas kernels  34.7 us (95%)
  other arithmetic  1.62 us (4%)
    pallas_call x1, Pallas kernels, per_device(): pl.pallas_call(functools.partial(kernel, n, m), name='galerkin', out_shap...  34.7 us
    div x1, other arithmetic, per_device(): return galerkin / bound  1.62 us

profile of v3, /device:TPU:0, one launch (start us, length us, event | category | flops | bytes accessed | tf_op | source)
XLA Modules:
  0.0 36.3 jit_solution(1185202685086629274)
XLA Ops:
  0.0 34.7 %galerkin.1 = (f32[2,16,128,128]{3,2,1,0:T(8,128)S(1)}, f32[128,128]{1,0:T(8,128)S(1)}) custom-call(f32[8,8,128,128]{3,2,1,0:T(8,128)} %blocks_ref.1, f32[8,128,128]{2,1,0:T(8,128)} %prolong_ref.1, s32[8,8]{1,0:T(8,128)} %cols_ref.1, s32[1,8]{1,0:T(1,128)} %bitcast.2, s32[1,8]{1,0:T(1,128)} %bitcast.3), custom_call_target="tpu_custom_call" | custom-call | tf_op jit(solution)/shard_map/galerkin/pallas_call | solution.py:446
  34.7 1.6 %broadcast_divide_fusion = f32[2,16,128,128]{3,2,1,0:T(8,128)} fusion(f32[2,16,128,128]{3,2,1,0:T(8,128)S(1)} %get-tuple-element.7, f32[128,128]{1,0:T(8,128)S(1)} %get-tuple-element.8), kind=kLoop, calls=%fused_computation | loop fusion | flops 524288 | bytes 4259840 | tf_op jit(solution)/shard_map/div | solution.py:493

commit v4 on v3

--- a/solution.py
+++ b/solution.py
@@ -85,8 +85,6 @@
         pltpu.make_async_copy(src, dst, small_sem.at[at])
         for at, (src, dst) in enumerate(
             (
-                (cols_ref, ask.at[pl.ds(0, rows)]),
-                (agg_ref, ask.at[pl.ds(rows, 1)]),
                 (cols_ref, cols_s),
                 (agg_ref, agg_s),
                 (counts_ref, counts_s),
@@ -151,6 +149,13 @@
 
     for copy in small:
         copy.wait()
+    at_lane = lax.broadcasted_iota(I32, ask.shape, 1)
+    asking = jnp.full(ask.shape, -1, I32)
+    for i in range(rows):
+        for k in range(slots):
+            asking = jnp.where(at_lane == i * slots + k, cols_s[i, k], asking)
+        asking = jnp.where(at_lane == none + i, agg_s[0, i], asking)
+    ask[...] = asking
 
     @pl.when(inner)
     def _():
@@ -189,8 +194,8 @@
         load_prolong.wait()
 
     def bounds(to, owner):
-        asked = ask_all[to][:rows]
-        mine = asked // rows == owner
+        asked = ask_all[to]
+        mine = (asked // rows == owner) & (at_lane < none)
         within = lax.rem(asked, rows)
         return jnp.min(jnp.where(mine, within, rows - 1)), jnp.max(jnp.where(mine, within, 0))
 
@@ -306,8 +311,6 @@
 
     lax.fori_loop(0, rows, first_product, 0)
 
-    spot = lax.broadcasted_iota(I32, (1, rows), 1)
-
     def second_product(owner):
         lhs = jnp.concatenate(
             [
@@ -316,10 +319,10 @@
             ],
             axis=0,
         )
-        ids = ask_all[owner][rows:]
+        ids = ask_all[owner]
         right = []
         for r in range(CAP):
-            one = jnp.max(jnp.where(spot == table_s[16 + r, owner], ids, 0)).astype(F32)
+            one = jnp.max(jnp.where(at_lane == none + table_s[16 + r, owner], ids, 0)).astype(F32)
             p = got[owner, r]
             right.append(jnp.concatenate([p * (1.0 - one), p * one], axis=1))
         rhs = jnp.concatenate(right, axis=0)
@@ -453,11 +456,11 @@
         in_specs=[hbm] * 5,
         out_specs=(vmem, vmem),
         scratch_shapes=[
-            pltpu.VMEM((rows + 1, slots), I32),
+            pltpu.VMEM((1, pl.cdiv(rows * slots + rows, 128) * 128), I32),
             pltpu.SMEM((rows, slots), I32),
             pltpu.SMEM((1, rows), I32),
             pltpu.SMEM((1, rows), I32),
-            dma((5,)),
+            dma((3,)),
             pltpu.VMEM((rows, slots, tile, tile), F32),
             pltpu.VMEM((rows, tile, tile), F32),
             pltpu.VMEM((rows * slots + 1, tile, tile), F32),
@@ -466,7 +469,7 @@
             pltpu.VMEM((n, CAP, tile, tile), F32),
             pltpu.VMEM((rows, tile // 2, tile), F32),
             pltpu.VMEM((n, CAP, tile // 2, tile), F32),
-            pltpu.VMEM((n, rows + 1, slots), I32),
+            pltpu.VMEM((n, 1, pl.cdiv(rows * slots + rows, 128) * 128), I32),
             pltpu.VMEM((AGD * tile, tile), F32),
             pltpu.VMEM((1, 128), F32),
             pltpu.VMEM((n * m, 1, 128), F32),

time: 36.5 us -> 35.8 us (0.981)
  Pallas kernels: 34.7 us -> 34 us
    pallas_call x1, Pallas kernels: 34.7 us -> 34 us  [per_device(): pl.pallas_call(functools.partial(kernel, n, m), name='galerkin', out_shap...]
where the time goes in v4:
time: 35.8 us; the launch traced here: 35.6 us
  Pallas kernels  34 us (95%)
  other arithmetic  1.62 us (5%)
    pallas_call x1, Pallas kernels, per_device(): pl.pallas_call(functools.partial(kernel, n, m), name='galerkin', out_shap...  34 us
    div x1, other arithmetic, per_device(): return galerkin / bound  1.62 us

profile of v4, /device:TPU:0, one launch (start us, length us, event | category | flops | bytes accessed | tf_op | source)
XLA Modules:
  0.0 35.6 jit_solution(12780198514134815887)
XLA Ops:
  0.0 34.0 %galerkin.1 = (f32[2,16,128,128]{3,2,1,0:T(8,128)S(1)}, f32[128,128]{1,0:T(8,128)S(1)}) custom-call(f32[8,8,128,128]{3,2,1,0:T(8,128)} %blocks_ref.1, f32[8,128,128]{2,1,0:T(8,128)} %prolong_ref.1, s32[8,8]{1,0:T(8,128)} %cols_ref.1, s32[1,8]{1,0:T(1,128)} %bitcast.2, s32[1,8]{1,0:T(1,128)} %bitcast.3), custom_call_target="tpu_custom_call" | custom-call | tf_op jit(solution)/shard_map/galerkin/pallas_call | solution.py:449
  34.0 1.6 %broadcast_divide_fusion = f32[2,16,128,128]{3,2,1,0:T(8,128)} fusion(f32[2,16,128,128]{3,2,1,0:T(8,128)S(1)} %get-tuple-element.7, f32[128,128]{1,0:T(8,128)S(1)} %get-tuple-element.8), kind=kLoop, calls=%fused_computation | loop fusion | flops 524288 | bytes 4259840 | tf_op jit(solution)/shard_map/div | solution.py:496

commit v5 on v4

--- a/solution.py
+++ b/solution.py
@@ -96,41 +96,54 @@
     for copy in small:
         copy.start()
 
-    def load_block(i):
-        return pltpu.make_async_copy(blocks_ref.at[i], blocks.at[i], block_sem.at[i])
-
-    def send_ask(to, slot):
+    load_blocks = pltpu.make_async_copy(blocks_ref, blocks, block_sem)
+
+    def send_ask(to, at):
         return pltpu.make_async_remote_copy(
-            ask, ask_all.at[slot], ask_send.at[to], ask_recv.at[slot], device_id={"col": to}
-        )
+            ask, ask_all.at[me], ask_send, ask_recv.at[at], device_id={"col": to}
+        )
+
+    def bytes_of(ref, send, recv):
+        return pltpu.make_async_remote_copy(ref, ref, send, recv, device_id={"col": across(1)})
+
+    def heard(at, count):
+        bytes_of(ask_all.at[pl.ds(0, count)], ask_send, ask_recv.at[at]).wait_recv()
+
+    def lane_of(owner):
+        return lax.rem(owner, width)
+
+    def near_at(owner):
+        return 1 + lane_of(owner)
+
+    def far_at(owner, far):
+        return 1 + (1 + far) * width + lane_of(owner)
 
     def send_push(part):
         some = (pl.ds(0, lead), pl.ds(lead, cut - lead))[part]
         return pltpu.make_async_remote_copy(
-            prolong.at[:, some], pushed.at[:, some], push_send.at[part], push_recv.at[part],
+            prolong.at[:, some], pushed.at[:, some], push_send, push_recv,
             device_id={"col": facing(0, 0)},
         )
 
-    def send_tiles(to, slot):
+    def send_tiles(to, slot, at):
         return pltpu.make_async_remote_copy(
-            sent.at[to], got.at[slot], tile_send.at[to], tile_recv.at[slot], device_id={"col": to}
+            sent.at[to], got.at[slot], tile_send, tile_recv.at[at], device_id={"col": to}
         )
 
     def send_rest(to, slot):
         rest = pl.ds(cut, tile - cut)
         return pltpu.make_async_remote_copy(
-            sent.at[to, :, rest], got.at[slot, :, rest], tile_send.at[to], tile_recv.at[slot],
+            sent.at[to, :, rest], got.at[slot, :, rest], tile_send, tile_recv.at[far_at(slot, 0)],
             device_id={"col": to},
         )
 
     def send_relay(to, slot):
         return pltpu.make_async_remote_copy(
-            passed.at[to], got.at[slot, :, pl.ds(0, cut)], relay_send.at[to], relay_recv.at[slot],
-            device_id={"col": to},
-        )
-
-    def ask_for(to):
-        send_ask(to, me).start()
+            passed.at[to], got.at[slot, :, pl.ds(0, cut)], relay_send, relay_recv, device_id={"col": to}
+        )
+
+    def ask_for(group):
+        return lambda to: send_ask(to, group).start()
 
     def tell(to, at):
         pl.semaphore_signal(known.at[at], inc=1, device_id={"col": to})
@@ -159,35 +172,33 @@
 
     @pl.when(inner)
     def _():
-        ask_for(facing(0, 0))
-        each(own, 0, 1, ask_for)
+        send_ask(facing(0, 0), 1).start()
+        each(own, 0, 1, ask_for(0))
         pl.semaphore_wait(known.at[0], 1)
         tell(facing(0, 0), 1)
         tell(own(1, 0), 0)
-        each(own, 1, 0, ask_for)
+        each(own, 1, 0, ask_for(3 + y))
         pl.semaphore_wait(known.at[1], 1)
         tell(own(1, 0), 0)
-        each(facing, 0, 1, ask_for)
+        each(facing, 0, 1, ask_for(1))
         pl.semaphore_wait(known.at[1], 1)
         tell(own(1, 0), 0)
-        each(facing, 1, 0, ask_for)
+        each(facing, 1, 0, ask_for(2))
         send_push(1).start()
 
     @pl.when(outer)
     def _():
-        ask_for(own(0, 0))
-        each(own, 1, 1, ask_for)
+        send_ask(own(0, 0), 3 + y).start()
+        each(own, 1, 1, ask_for(0))
         pl.semaphore_wait(known.at[0], 1)
-        ask_for(facing(0, 0))
-        each(own, 0, 1, ask_for)
+        send_ask(facing(0, 0), 2).start()
+        each(own, 0, 1, ask_for(3 + y))
         pl.semaphore_wait(known.at[0], 1)
-        each(facing, 0, 1, ask_for)
+        each(facing, 0, 1, ask_for(2))
         pl.semaphore_wait(known.at[0], 1)
-        each(facing, 1, 0, ask_for)
-
-    @pl.loop(0, rows)
-    def _(i):
-        load_block(i).start()
+        each(facing, 1, 0, ask_for(1))
+
+    load_blocks.start()
 
     @pl.when(outer)
     def _():
@@ -199,33 +210,48 @@
         within = lax.rem(asked, rows)
         return jnp.min(jnp.where(mine, within, rows - 1)), jnp.max(jnp.where(mine, within, 0))
 
-    def reply(to):
-        send_ask(to, to).wait_recv()
+    def reply(to, at):
         low, high = bounds(to, me)
         sent[to, 0] = prolong[low]
         sent[to, 1] = prolong[high]
-        send_tiles(to, me).start()
+        send_tiles(to, me, at).start()
+
+    def reply_line(to):
+        reply(to, 0)
+
+    def reply_near(to):
+        heard(3 + lane_of(to), 1)
+        reply(to, near_at(me))
+
+    def reply_far(to):
+        reply(to, far_at(me, 1))
 
     def reply_rest(to):
-        send_ask(to, to).wait_recv()
         low, high = bounds(to, me)
         sent[to, 0, cut:] = prolong[low][cut:]
         sent[to, 1, cut:] = prolong[high][cut:]
         send_rest(to, me).start()
 
-    @pl.when(inner)
-    def _():
-        each(own, 0, 1, reply)
-        each(own, 1, 0, reply)
+    if width > 1:
+        heard(0, width - 1)
+
+    @pl.when(inner)
+    def _():
+        each(own, 0, 1, reply_line)
+        each(own, 1, 0, reply_near)
+        heard(2, width)
         each(facing, 1, 0, reply_rest)
+        heard(1, width)
         each(facing, 0, 0, reply_rest)
 
     @pl.when(outer)
     def _():
-        each(own, 1, 1, reply)
-        each(own, 0, 0, reply)
-        each(facing, 1, 0, reply)
-        each(facing, 0, 0, reply)
+        each(own, 1, 1, reply_line)
+        each(own, 0, 0, reply_near)
+        heard(1, width)
+        each(facing, 1, 0, reply_far)
+        heard(2, width)
+        each(facing, 0, 0, reply_far)
 
     sub = lax.broadcasted_iota(I32, (8, 128), 0)
     lane = lax.broadcasted_iota(I32, (8, 128), 1)
@@ -279,8 +305,7 @@
 
     @pl.when(inner)
     def _():
-        send_push(0).wait_recv()
-        send_push(1).wait_recv()
+        bytes_of(pushed, push_send, push_recv).wait_recv()
         face = facing(0, 0)
 
         def relay(to):
@@ -294,8 +319,9 @@
         got[face, 0, :cut] = pushed[table_s[16, face]]
         got[face, 1, :cut] = pushed[table_s[17, face]]
 
+    load_blocks.wait()
+
     def first_product(i, _):
-        load_block(i).wait()
         ph, pw = halves(prolong[i].T)
         lhs = jnp.concatenate([ph, pw, ph], axis=1)
         for k in range(0, slots, 2):
@@ -339,38 +365,38 @@
 
     second_product(me)
 
-    def collect(owner):
-        send_tiles(owner, owner).wait_recv()
+    def collect_near(owner):
+        send_tiles(owner, owner, near_at(owner)).wait_recv()
         second_product(owner)
 
-    def collect_parts(owner):
-        send_relay(owner, owner).wait_recv()
+    def collect_far(owner):
+        send_tiles(owner, owner, far_at(owner, 1)).wait_recv()
+        second_product(owner)
+
+    def collect_rest(owner):
         send_rest(owner, owner).wait_recv()
         second_product(owner)
 
-    @pl.when(inner)
-    def _():
-        each(own, 0, 1, collect)
-        each(own, 1, 0, collect)
+    if width > 1:
+        bytes_of(got.at[pl.ds(0, width - 1)], tile_send, tile_recv.at[0]).wait_recv()
+
+    @pl.when(inner)
+    def _():
+        each(own, 0, 1, second_product)
+        each(own, 1, 0, collect_near)
+        each(facing, 1, 0, collect_far)
+        if width > 1:
+            bytes_of(passed.at[pl.ds(0, width - 1)], relay_send, relay_recv).wait_recv()
 
     @pl.when(outer)
     def _():
-        each(own, 1, 1, collect)
-        each(own, 0, 0, collect)
-
-    each(facing, 1, 0, collect)
-
-    @pl.when(inner)
-    def _():
-        send_rest(facing(0, 0), facing(0, 0)).wait_recv()
-
-    @pl.when(outer)
-    def _():
-        send_relay(facing(0, 0), facing(0, 0)).wait_recv()
-        send_rest(facing(0, 0), facing(0, 0)).wait_recv()
-
-    second_product(facing(0, 0))
-    each(facing, 0, 1, collect_parts)
+        each(own, 1, 1, second_product)
+        collect_near(own(0, 0))
+        each(facing, 1, 0, collect_far)
+        each(own, 0, 1, collect_near)
+        bytes_of(passed.at[pl.ds(0, width)], relay_send, relay_recv).wait_recv()
+
+    each(facing, 0, 0, collect_rest)
 
     most = jnp.max(jnp.sum(rowsum[...], axis=1, keepdims=True), axis=0, keepdims=True)
     place_all = my_row * n + me
@@ -401,36 +427,17 @@
         peaks.at[others], peaks.at[others], peak_send, peak_recv, device_id={"col": across(1)}
     )
 
-    @pl.loop(1, n)
-    def _(off):
-        send_ask(across(off), me).wait_send()
-
-    def sent_whole(to):
-        send_tiles(to, me).wait_send()
-
-    def sent_rest(to):
-        send_rest(to, me).wait_send()
-
-    def sent_relay(to):
-        send_relay(to, me).wait_send()
-
-    @pl.when(inner)
-    def _():
-        send_push(0).wait_send()
-        send_push(1).wait_send()
-        each(own, 0, 1, sent_whole)
-        each(own, 0, 1, sent_relay)
-        each(own, 1, 0, sent_whole)
-        each(own, 1, 0, sent_relay)
-        each(facing, 0, 0, sent_rest)
-        each(facing, 1, 0, sent_rest)
+    bytes_of(ask_all.at[pl.ds(0, n - 1)], ask_send, ask_recv.at[0]).wait_send()
+
+    @pl.when(inner)
+    def _():
+        bytes_of(pushed, push_send, push_recv).wait_send()
+        bytes_of(passed.at[pl.ds(0, 2 * width - 1)], relay_send, relay_recv).wait_send()
+        bytes_of(sent.at[pl.ds(0, 3 * width - 1)], tile_send, tile_recv.at[0]).wait_send()
 
     @pl.when(outer)
     def _():
-        each(own, 1, 1, sent_whole)
-        each(own, 0, 0, sent_whole)
-        each(facing, 0, 0, sent_whole)
-        each(facing, 1, 0, sent_whole)
+        bytes_of(sent.at[pl.ds(0, n - 1)], tile_send, tile_recv.at[0]).wait_send()
 
     every.wait_send()
     every.wait_recv()
@@ -474,17 +481,17 @@
             pltpu.VMEM((1, 128), F32),
             pltpu.VMEM((n * m, 1, 128), F32),
             pltpu.SMEM((24, 128), I32),
-            dma((rows,)),
-            dma,
-            dma,
-            dma((n,)),
-            dma((n,)),
-            dma((n,)),
-            dma((n,)),
-            dma((n,)),
-            dma((n,)),
-            dma((2,)),
-            dma((2,)),
+            dma,
+            dma,
+            dma,
+            dma,
+            dma((3 + n // 4,)),
+            dma,
+            dma((1 + 3 * (n // 4),)),
+            dma,
+            dma,
+            dma,
+            dma,
             dma,
             dma,
             pltpu.SemaphoreType.REGULAR((2,)),

time: 35.8 us -> 35.3 us (0.986)
  Pallas kernels: 34 us -> 33.6 us
    pallas_call x1, Pallas kernels: 34 us -> 33.6 us  [per_device(): pl.pallas_call(functools.partial(kernel, n, m), name='galerkin', out_shap...]
where the time goes in v5:
time: 35.3 us; the launch traced here: 35.2 us
  Pallas kernels  33.6 us (95%)
  other arithmetic  1.62 us (5%)
    pallas_call x1, Pallas kernels, per_device(): pl.pallas_call(functools.partial(kernel, n, m), name='galerkin', out_shap...  33.6 us
    div x1, other arithmetic, per_device(): return galerkin / bound  1.62 us

profile of v5, /device:TPU:0, one launch (start us, length us, event | category | flops | bytes accessed | tf_op | source)
XLA Modules:
  0.0 35.2 jit_solution(5683823286354790252)
XLA Ops:
  0.0 33.6 %galerkin.1 = (f32[2,16,128,128]{3,2,1,0:T(8,128)S(1)}, f32[128,128]{1,0:T(8,128)S(1)}) custom-call(f32[8,8,128,128]{3,2,1,0:T(8,128)} %blocks_ref.1, f32[8,128,128]{2,1,0:T(8,128)} %prolong_ref.1, s32[8,8]{1,0:T(8,128)} %cols_ref.1, s32[1,8]{1,0:T(1,128)} %bitcast.2, s32[1,8]{1,0:T(1,128)} %bitcast.3), custom_call_target="tpu_custom_call" | custom-call | tf_op jit(solution)/shard_map/galerkin/pallas_call | solution.py:456
  33.6 1.6 %broadcast_divide_fusion = f32[2,16,128,128]{3,2,1,0:T(8,128)} fusion(f32[2,16,128,128]{3,2,1,0:T(8,128)S(1)} %get-tuple-element.7, f32[128,128]{1,0:T(8,128)S(1)} %get-tuple-element.8), kind=kLoop, calls=%fused_computation | loop fusion | flops 524288 | bytes 4259840 | tf_op jit(solution)/shard_map/div | solution.py:503

commit v6 on v5

--- a/solution.py
+++ b/solution.py
@@ -27,7 +27,7 @@
     n, m, blocks_ref, prolong_ref, cols_ref, agg_ref, counts_ref,
     out_ref, bound_ref,
     ask, cols_s, agg_s, counts_s, small_sem,
-    blocks, prolong, partial, table, sent, got, pushed, passed, ask_all, rowsum, peak, peaks, table_s,
+    blocks, prolong, partial, table, sent, got, pushed, passed, mask, early, left, ask_all, rowsum, peak, peaks, table_s,
     block_sem, prolong_sem, table_sem, ask_send, ask_recv,
     tile_send, tile_recv, relay_send, relay_recv, push_send, push_recv,
     peak_send, peak_recv, known,
@@ -363,6 +363,57 @@
                     c * tile : (c + 1) * tile, a * tile : (a + 1) * tile
                 ]
 
+    def three(x, y):
+        return jnp.concatenate([x, y, x], axis=1)
+
+    def deep_three(x, y):
+        return jnp.concatenate([x, x, y], axis=0)
+
+    def masked(owner, at, some):
+        right = []
+        for r in range(CAP):
+            p = got[owner, r, some]
+            right.append(jnp.concatenate([p, p], axis=1) * mask[at, r])
+        return deep_three(*halves(jnp.concatenate(right, axis=0)))
+
+    def prepare(owner):
+        at = lax.rem(owner, width)
+        ids = ask_all[owner]
+        for r in range(CAP):
+            one = jnp.max(jnp.where(at_lane == none + table_s[16 + r, owner], ids, 0)).astype(F32)
+            second = (lax.broadcasted_iota(I32, (1, 2 * tile), 1) >= tile).astype(F32)
+            mask[at, r] = second * one + (1.0 - second) * (1.0 - one)
+        for part in range(2):
+            lhs = jnp.concatenate(
+                [
+                    jnp.concatenate(
+                        [
+                            partial[table_s[8 + c * CAP + r, owner]][:, part * cut : (part + 1) * cut]
+                            for r in range(CAP)
+                        ],
+                        axis=1,
+                    )
+                    for c in range(AGD)
+                ],
+                axis=0,
+            )
+            wide = three(*halves(lhs))
+            if part == 0:
+                early[at] = dot(wide, masked(owner, at, slice(0, cut)))
+            else:
+                left[at] = wide
+
+    def finish(owner):
+        at = lax.rem(owner, width)
+        prod = early[at] + dot(left[at], masked(owner, at, slice(cut, tile)))
+        size = jnp.abs(prod)
+        rowsum[...] += size[:, :tile] + size[:, tile:]
+        for c in range(AGD):
+            for a in range(AGD):
+                out_ref[c, owner * AGD + a] = prod[
+                    c * tile : (c + 1) * tile, a * tile : (a + 1) * tile
+                ]
+
     second_product(me)
 
     def collect_near(owner):
@@ -375,7 +426,7 @@
 
     def collect_rest(owner):
         send_rest(owner, owner).wait_recv()
-        second_product(owner)
+        finish(owner)
 
     if width > 1:
         bytes_of(got.at[pl.ds(0, width - 1)], tile_send, tile_recv.at[0]).wait_recv()
@@ -383,10 +434,11 @@
     @pl.when(inner)
     def _():
         each(own, 0, 1, second_product)
+        if width > 1:
+            bytes_of(passed.at[pl.ds(0, width - 1)], relay_send, relay_recv).wait_recv()
+        each(facing, 0, 0, prepare)
         each(own, 1, 0, collect_near)
         each(facing, 1, 0, collect_far)
-        if width > 1:
-            bytes_of(passed.at[pl.ds(0, width - 1)], relay_send, relay_recv).wait_recv()
 
     @pl.when(outer)
     def _():
@@ -395,6 +447,7 @@
         each(facing, 1, 0, collect_far)
         each(own, 0, 1, collect_near)
         bytes_of(passed.at[pl.ds(0, width)], relay_send, relay_recv).wait_recv()
+        each(facing, 0, 0, prepare)
 
     each(facing, 0, 0, collect_rest)
 
@@ -442,7 +495,7 @@
     every.wait_send()
     every.wait_recv()
     bound_ref[...] = jnp.broadcast_to(
-        jnp.max(peaks[...], axis=0)[:1, :1] + 1e-06, bound_ref.shape
+        1.0 / (jnp.max(peaks[...], axis=0)[:1, :1] + 1e-06), bound_ref.shape
     )
 
 
@@ -476,6 +529,9 @@
             pltpu.VMEM((n, CAP, tile, tile), F32),
             pltpu.VMEM((rows, tile // 2, tile), F32),
             pltpu.VMEM((n, CAP, tile // 2, tile), F32),
+            pltpu.VMEM((n // 4, CAP, 1, 2 * tile), F32),
+            pltpu.VMEM((n // 4, AGD * tile, AGD * tile), F32),
+            pltpu.VMEM((n // 4, AGD * tile, 3 * CAP * (tile // 2)), BF16),
             pltpu.VMEM((n, 1, pl.cdiv(rows * slots + rows, 128) * 128), I32),
             pltpu.VMEM((AGD * tile, tile), F32),
             pltpu.VMEM((1, 128), F32),
@@ -500,7 +556,7 @@
             collective_id=0, has_side_effects=True, vmem_limit_bytes=48 * 1024 * 1024
         ),
     )(*(pltpu.with_memory_space_constraint(x, pltpu.HBM) for x in (blocks, prolong, columns, agg_row, counts.reshape(1, rows))))
-    return galerkin / bound
+    return galerkin * bound
 
 
 def solution(mesh):

time: 35.3 us -> 35 us (level)
    div x1 -> x0, other arithmetic: 1.62 us -> none  [per_device(): return galerkin / bound]
    mul x0 -> x1, other arithmetic: none -> 1.55 us  [per_device(): return galerkin * bound]
where the time goes in v6:
time: 35 us; the launch traced here: 34.9 us
  Pallas kernels  33.3 us (95%)
  other arithmetic  1.55 us (4%)
    pallas_call x1, Pallas kernels, per_device(): pl.pallas_call(functools.partial(kernel, n, m), name='galerkin', out_shap...  33.3 us
    mul x1, other arithmetic, per_device(): return galerkin * bound  1.55 us

profile of v6, /device:TPU:0, one launch (start us, length us, event | category | flops | bytes accessed | tf_op | source)
XLA Modules:
  0.0 34.9 jit_solution(428673907798776383)
XLA Ops:
  0.0 33.3 %galerkin.1 = (f32[2,16,128,128]{3,2,1,0:T(8,128)S(1)}, f32[128,128]{1,0:T(8,128)S(1)}) custom-call(f32[8,8,128,128]{3,2,1,0:T(8,128)} %blocks_ref.1, f32[8,128,128]{2,1,0:T(8,128)} %prolong_ref.1, s32[8,8]{1,0:T(8,128)} %cols_ref.1, s32[1,8]{1,0:T(1,128)} %bitcast.2, s32[1,8]{1,0:T(1,128)} %bitcast.3), custom_call_target="tpu_custom_call" | custom-call | tf_op jit(solution)/shard_map/galerkin/pallas_call | solution.py:509
  33.3 1.5 %broadcast_multiply_fusion = f32[2,16,128,128]{3,2,1,0:T(8,128)} fusion(f32[2,16,128,128]{3,2,1,0:T(8,128)S(1)} %get-tuple-element.7, f32[128,128]{1,0:T(8,128)S(1)} %get-tuple-element.8), kind=kLoop, calls=%fused_computation | loop fusion | flops 524288 | bytes 4259840 | tf_op jit(solution)/shard_map/mul | solution.py:559

commit v7 on v6

--- a/solution.py
+++ b/solution.py
@@ -152,9 +152,9 @@
 
     @pl.when(inner)
     def _():
-        tell(facing(0, 0), 1)
         load_prolong.wait()
         send_push(0).start()
+        tell(facing(0, 0), 1)
 
     @pl.when(outer)
     def _():
@@ -242,7 +242,8 @@
         heard(2, width)
         each(facing, 1, 0, reply_rest)
         heard(1, width)
-        each(facing, 0, 0, reply_rest)
+        each(facing, 0, 1, reply_rest)
+        reply_rest(facing(0, 0))
 
     @pl.when(outer)
     def _():
@@ -449,7 +450,8 @@
         bytes_of(passed.at[pl.ds(0, width)], relay_send, relay_recv).wait_recv()
         each(facing, 0, 0, prepare)
 
-    each(facing, 0, 0, collect_rest)
+    each(facing, 0, 1, collect_rest)
+    collect_rest(facing(0, 0))
 
     most = jnp.max(jnp.sum(rowsum[...], axis=1, keepdims=True), axis=0, keepdims=True)
     place_all = my_row * n + me

time: 35 us -> 35 us (level)
  no operation moved by 1% of the time
where the time goes in v7:
time: 35 us; the launch traced here: 34.8 us
  Pallas kernels  33.3 us (95%)
  other arithmetic  1.55 us (4%)
    pallas_call x1, Pallas kernels, per_device(): pl.pallas_call(functools.partial(kernel, n, m), name='galerkin', out_shap...  33.3 us
    mul x1, other arithmetic, per_device(): return galerkin * bound  1.55 us

profile of v7, /device:TPU:0, one launch (start us, length us, event | category | flops | bytes accessed | tf_op | source)
XLA Modules:
  0.0 34.8 jit_solution(16740994376862085491)
XLA Ops:
  0.0 33.3 %galerkin.1 = (f32[2,16,128,128]{3,2,1,0:T(8,128)S(1)}, f32[128,128]{1,0:T(8,128)S(1)}) custom-call(f32[8,8,128,128]{3,2,1,0:T(8,128)} %blocks_ref.1, f32[8,128,128]{2,1,0:T(8,128)} %prolong_ref.1, s32[8,8]{1,0:T(8,128)} %cols_ref.1, s32[1,8]{1,0:T(1,128)} %bitcast.2, s32[1,8]{1,0:T(1,128)} %bitcast.3), custom_call_target="tpu_custom_call" | custom-call | tf_op jit(solution)/shard_map/galerkin/pallas_call | solution.py:511
  33.3 1.5 %broadcast_multiply_fusion = f32[2,16,128,128]{3,2,1,0:T(8,128)} fusion(f32[2,16,128,128]{3,2,1,0:T(8,128)S(1)} %get-tuple-element.7, f32[128,128]{1,0:T(8,128)S(1)} %get-tuple-element.8), kind=kLoop, calls=%fused_computation | loop fusion | flops 524288 | bytes 4259840 | tf_op jit(solution)/shard_map/mul | solution.py:561

commit v8 on v6

--- a/solution.py
+++ b/solution.py
@@ -63,6 +63,12 @@
         def _(off):
             act(where(far, off))
 
+    load_lead, load_tail = (
+        pltpu.make_async_copy(prolong_ref.at[:, some], prolong.at[:, some], prolong_sem.at[at])
+        for at, some in enumerate((pl.ds(0, lead), pl.ds(lead, tile - lead)))
+    )
+    load_lead.start()
+
     barrier = pltpu.get_barrier_semaphore()
 
     def greet(to):
@@ -91,8 +97,7 @@
             )
         )
     ]
-    load_prolong = pltpu.make_async_copy(prolong_ref, prolong, prolong_sem)
-    load_prolong.start()
+    load_tail.start()
     for copy in small:
         copy.start()
 
@@ -153,7 +158,7 @@
     @pl.when(inner)
     def _():
         tell(facing(0, 0), 1)
-        load_prolong.wait()
+        load_lead.wait()
         send_push(0).start()
 
     @pl.when(outer)
@@ -184,6 +189,7 @@
         pl.semaphore_wait(known.at[1], 1)
         tell(own(1, 0), 0)
         each(facing, 1, 0, ask_for(2))
+        load_tail.wait()
         send_push(1).start()
 
     @pl.when(outer)
@@ -202,7 +208,8 @@
 
     @pl.when(outer)
     def _():
-        load_prolong.wait()
+        load_lead.wait()
+        load_tail.wait()
 
     def bounds(to, owner):
         asked = ask_all[to]
@@ -538,7 +545,7 @@
             pltpu.VMEM((n * m, 1, 128), F32),
             pltpu.SMEM((24, 128), I32),
             dma,
-            dma,
+            dma((2,)),
             dma,
             dma,
             dma((3 + n // 4,)),

time: 35 us -> 35 us (level)
  no operation moved by 1% of the time
where the time goes in v8:
time: 35 us; the launch traced here: 34.9 us
  Pallas kernels  33.3 us (95%)
  other arithmetic  1.55 us (4%)
    pallas_call x1, Pallas kernels, per_device(): pl.pallas_call(functools.partial(kernel, n, m), name='galerkin', out_shap...  33.3 us
    mul x1, other arithmetic, per_device(): return galerkin * bound  1.55 us

profile of v8, /device:TPU:0, one launch (start us, length us, event | category | flops | bytes accessed | tf_op | source)
XLA Modules:
  0.0 34.9 jit_solution(495568315234268102)
XLA Ops:
  0.0 33.3 %galerkin.1 = (f32[2,16,128,128]{3,2,1,0:T(8,128)S(1)}, f32[128,128]{1,0:T(8,128)S(1)}) custom-call(f32[8,8,128,128]{3,2,1,0:T(8,128)} %blocks_ref.1, f32[8,128,128]{2,1,0:T(8,128)} %prolong_ref.1, s32[8,8]{1,0:T(8,128)} %cols_ref.1, s32[1,8]{1,0:T(1,128)} %bitcast.2, s32[1,8]{1,0:T(1,128)} %bitcast.3), custom_call_target="tpu_custom_call" | custom-call | tf_op jit(solution)/shard_map/galerkin/pallas_call | solution.py:516
  33.3 1.5 %broadcast_multiply_fusion = f32[2,16,128,128]{3,2,1,0:T(8,128)} fusion(f32[2,16,128,128]{3,2,1,0:T(8,128)S(1)} %get-tuple-element.7, f32[128,128]{1,0:T(8,128)S(1)} %get-tuple-element.8), kind=kLoop, calls=%fused_computation | loop fusion | flops 524288 | bytes 4259840 | tf_op jit(solution)/shard_map/mul | solution.py:566
